TPU v7x, 512 devices: a whole 4x8x8 slice. The times are simulated.
512 devices in a mesh: dp: 8 (over z_hi, core), fsdp: 16 (over z_lo, y), tp: 4 (over x).
Axes of the slice: x: 4, y: 8, z: 8 (z_hi: 4, z_lo: 2; z = z_hi * 2 + z_lo), core: 2. Of those that a mesh axis runs over, the one named last changes fastest.
Arguments:
- layer_input: bfloat16 [65536, 4096], P(('dp', 'fsdp'), 'tp'), may hold values from -24 to 24
- value_grad: bfloat16 [65536, 2048], P(('dp', 'fsdp'), 'tp'), may hold values from -6 to 6
- residual_grad: bfloat16 [65536, 4096], P(('dp', 'fsdp'), 'tp'), may hold values from -6 to 6
- value_weight: bfloat16 [4096, 2048], P(('tp', 'fsdp')), may hold values from -0.125 to 0.125
- owner: int32 [65536, 1], P(('dp', 'fsdp')), may hold values from 0 to 15; in each aligned block of 512 rows (0 to 511, 512 to 1023, ...) at most 64 rows name the same one
- key_row: int32 [65536], P(('dp', 'fsdp')), may hold values from 0 to 255
Outputs:
- weight_grad: float32 [4096, 2048], P(('tp', 'fsdp'))
- key_grad: float32 [4096, 4096], P('fsdp', 'tp')
Inputs may be any that keep to these rules, and one draw needn't show every extreme that they name: Among the 512 tokens of one device (aligned blocks of rows) at most 64 name the same owner, and that bound is reached.
All inputs are finite; a program needn't handle non-finite values.
Results may differ from a plain program's by a relative error of at most 0.0029.
Values may be sent and summed in bfloat16 or wider, within the bound.
A program may use at most 64 MiB of HBM per device.

v0:
```python
import jax
import jax.numpy as jnp
from jax import lax
from jax.sharding import PartitionSpec as P

KEY_DEV = 256


def body(layer_input, value_grad, residual_grad, value_weight, owner, key_row):
    all_heads = lax.all_gather(value_grad, "tp", axis=1, tiled=True)
    tok_rows = layer_input.shape[0]
    features = layer_input.shape[1]
    groups = lax.axis_size("fsdp")
    slots = 2 * tok_rows // groups
    width = all_heads.shape[1]
    term = lax.dot_general(
        layer_input, all_heads, (((0,), (0,)), ((), ())), preferred_element_type=jnp.float32
    )
    pieces = term.astype(jnp.bfloat16).reshape(groups, features // groups, width)
    arrived = lax.all_to_all(pieces, "fsdp", split_axis=0, concat_axis=0, tiled=True)
    shard = jnp.sum(arrived.astype(jnp.float32), axis=0)
    back = lax.dot_general(
        all_heads,
        lax.all_gather(value_weight, "fsdp", axis=0, tiled=True),
        (((1,), (1,)), ((), ())),
        preferred_element_type=jnp.float32,
    )
    input_grad = (residual_grad.astype(jnp.float32) + back).astype(jnp.bfloat16)
    target = owner[:, 0]
    onehot = (target[:, None] == jnp.arange(groups, dtype=jnp.int32)[None, :]).astype(jnp.int32)
    position = jnp.sum(jnp.cumsum(onehot, axis=0) * onehot, axis=1) - 1
    outgoing = (
        jnp.zeros((groups, slots, features), jnp.bfloat16).at[target, position].set(input_grad)
    )
    out_keys = jnp.full((groups, slots), -1, jnp.int32).at[target, position].set(key_row)
    arrived = lax.all_to_all(outgoing, "fsdp", split_axis=0, concat_axis=0, tiled=True)
    arrived_keys = lax.all_to_all(out_keys, "fsdp", split_axis=0, concat_axis=0, tiled=True)
    flat_rows = arrived.reshape(groups * slots, features)
    selector = (
        arrived_keys.reshape(groups * slots)[:, None]
        == jnp.arange(KEY_DEV, dtype=jnp.int32)[None, :]
    ).astype(jnp.bfloat16)
    table = lax.dot_general(
        selector, flat_rows, (((0,), (0,)), ((), ())), preferred_element_type=jnp.float32
    )
    weight_grad = lax.psum(shard, "dp")
    key_grad = lax.psum(table, "dp")
    return (weight_grad, key_grad)


def solution(mesh):
    return jax.shard_map(
        body,
        mesh=mesh,
        in_specs=(
            P(("dp", "fsdp"), "tp"),
            P(("dp", "fsdp"), "tp"),
            P(("dp", "fsdp"), "tp"),
            P(("tp", "fsdp"), None),
            P(("dp", "fsdp"), None),
            P(("dp", "fsdp")),
        ),
        out_specs=(P(("tp", "fsdp"), None), P("fsdp", "tp")),
        check_vma=False,
    )
```

profile of v0, /device:TPU:1, one launch (start us, length us, event | category | flops | bytes accessed | tf_op | source)
XLA Modules:
  0.0 392.0 jit_solution(7241025913781372780)
XLA Ops:
  7.2 0.0 copy-start
  7.2 0.0 all-gather.3.cloned.1.call-start
  7.2 0.7 all-gather.3.cloned.1.call-update
  7.9 0.0 all-gather.5.cloned.1.call-start
  8.0 0.7 all-gather.5.cloned.1.call-update
  8.7 0.7 fusion.4
  9.4 1.1 reduce-window.6
  10.5 0.2 slice_reduce_fusion
  10.7 0.8 fusion.3
  11.5 0.7 or_select_fusion
  12.2 0.6 broadcast_in_dim.4
  12.8 71.1 %scatter_fusion = s32[16,64]{1,0:T(8,128)} fusion(s32[16,64]{1,0:T(8,128)} %broadcast_in_dim.4, s32[512]{0:T(512)S(1)} %bitcast.30, s32[512]{0:T(512)} %param.11), kind=kCustom, calls=%fused_computation | custom fusion | bytes 10240 | tf_op jit(solution)/shard_map/scatter | solution.py:35
  84.0 9.6 %all-to-all-start.1 = ((s32[16,1,64]{2,1,0:T(1,128)}), s32[16,1,64]{2,1,0:T(1,128)S(1)}, u32[]{:S(2)}, u32[]{:S(2)}) async-start(s32[16,1,64]{2,1,0:T(1,128)} %bitcast.8), calls=%async_computation.1 | async-start | bytes 16384 | tf_op jit(solution)/shard_map/all_to_all | solution.py:37
  93.6 0.0 all-gather.3.cloned.1.call-done
  93.6 0.0 copy-done
  93.6 6.0 %convolution_convert_fusion = bf16[1024,2048]{1,0:T(8,128)(2,1)} fusion(bf16[512,1024]{1,0:T(8,128)(2,1)S(1)} %copy-done, bf16[512,2048]{1,0:T(8,128)(2,1)} %all-gather.3.cloned.1.call-done), kind=kOutput, calls=%fused_computation.3 | convolution fusion | flops 2149580800 | bytes 7340032 | tf_op jit(solution)/shard_map/dot_general | solution.py:16
  99.6 1.3 all-to-all-done.1
  100.8 0.0 copy-start.1
  100.8 6.5 %all-to-all-start = ((bf16[16,64,2048]{2,1,0:T(8,128)(2,1)}), bf16[16,64,2048]{2,1,0:T(8,128)(2,1)}, u32[]{:S(2)}, u32[]{:S(2)}) async-start(bf16[16,64,2048]{2,1,0:T(8,128)(2,1)} %bitcast.32), calls=%async_computation | async-start | bytes 8388608 | tf_op jit(solution)/shard_map/all_to_all | solution.py:20
  107.3 50.5 %all-gather.5.cloned.1.call-done = bf16[1024,2048]{1,0:T(8,128)(2,1)} async-done(((bf16[64,2048]{1,0:T(8,128)(2,1)}), bf16[1024,2048]{1,0:T(8,128)(2,1)}) %all-gather.5.cloned.1.call-update) | async-done | bytes 4194320 | tf_op jit(solution)/shard_map/all_gather | solution.py:24
  157.8 0.0 copy-done.1
  157.8 5.2 %add_convert_fusion = bf16[512,1024]{1,0:T(8,128)(2,1)S(1)} fusion(bf16[512,1024]{1,0:T(8,128)(2,1)S(1)} %copy-done.1, bf16[512,2048]{1,0:T(8,128)(2,1)} %all-gather.3.cloned.1.call-done, bf16[1024,2048]{1,0:T(8,128)(2,1)} %all-gather.5.cloned.1.call-done), kind=kOutput, calls=%fused_computation.4 | convolution fusion | flops 2149056512 | bytes 8388608 | tf_op jit(solution)/shard_map/dot_general | solution.py:22
  163.0 1.7 broadcast_in_dim.5
  164.6 72.2 %scatter_fusion.1 = bf16[16,64,1024]{2,1,0:T(8,128)(2,1)} fusion(bf16[16,64,1024]{2,1,0:T(8,128)(2,1)} %broadcast_in_dim.5, s32[512]{0:T(512)S(1)} %bitcast.31, bf16[512,1024]{1,0:T(8,128)(2,1)S(1)} %add_convert_fusion), kind=kCustom, calls=%fused_computation.1 | custom fusion | bytes 3149824 | tf_op jit(solution)/shard_map/scatter | solution.py:33
  236.8 0.0 all-to-all-done
  236.8 3.7 all-to-all-start.2
  240.6 0.0 all-reduce.3.cloned.1.call-start
  240.6 0.5 broadcast.102
  241.1 0.7 reduce.5
  241.8 0.1 eq.48
  241.9 3.8 convert_reduce_fusion
  245.7 22.4 %all-to-all-done.2 = bf16[16,64,1024]{2,1,0:T(8,128)(2,1)S(1)} async-done(((bf16[16,64,1024]{2,1,0:T(8,128)(2,1)}), bf16[16,64,1024]{2,1,0:T(8,128)(2,1)S(1)}, u32[]{:S(2)}, u32[]{:S(2)}) %all-to-all-start.2) | async-done | bytes 2097184 | tf_op jit(solution)/shard_map/all_to_all | solution.py:36
  268.0 1.9 fusion
  270.0 0.0 all-reduce.3.cloned.1.call-update
  270.0 111.2 %all-reduce.3.cloned.1.call-done = (f32[64,2048]{1,0:T(8,128)}, f32[256,1024]{1,0:T(8,128)}) async-done(((f32[64,2048]{1,0:T(8,128)}, f32[256,1024]{1,0:T(8,128)}), (f32[64,2048]{1,0:T(8,128)}, f32[256,1024]{1,0:T(8,128)})) %all-reduce.3.cloned.1.call-update) | async-done | bytes 1572880 | tf_op jit(solution)/shard_map/psum | solution.py:46
  381.3 1.9 copy.17
  383.1 2.3 copy.18
  (3 shorter events, 0.0 us)
Async XLA Ops:
  7.2 86.4 %copy-start = (bf16[512,1024]{1,0:T(8,128)(2,1)S(1)}, bf16[512,1024]{1,0:T(8,128)(2,1)}, u32[]{:S(2)}) copy-start(bf16[512,1024]{1,0:T(8,128)(2,1)} %param.6) | copy-start | bytes 3145732
  7.2 86.4 %all-gather.3.cloned.1.call-start = ((), (), s32[]{:S(2)}) async-start(), calls=%async_computation.3 | async-start | bytes 2621440 | tf_op jit(solution)/shard_map/all_gather | solution.py:10
  7.9 149.9 %all-gather.5.cloned.1.call-start = ((), (), s32[]{:S(2)}) async-start(), calls=%async_computation.4 | async-start | bytes 4456448 | tf_op jit(solution)/shard_map/all_gather | solution.py:24
  84.0 16.9 %all-to-all-start.1 = ((s32[16,1,64]{2,1,0:T(1,128)}), s32[16,1,64]{2,1,0:T(1,128)S(1)}, u32[]{:S(2)}, u32[]{:S(2)}) async-start(s32[16,1,64]{2,1,0:T(1,128)} %bitcast.8), calls=%async_computation.1 | async-start | bytes 16384 | tf_op jit(solution)/shard_map/all_to_all | solution.py:37
  100.8 56.9 %copy-start.1 = (bf16[512,1024]{1,0:T(8,128)(2,1)S(1)}, bf16[512,1024]{1,0:T(8,128)(2,1)}, u32[]{:S(2)}) copy-start(bf16[512,1024]{1,0:T(8,128)(2,1)} %param.8) | copy-start | bytes 3145732
  100.8 136.0 %all-to-all-start = ((bf16[16,64,2048]{2,1,0:T(8,128)(2,1)}), bf16[16,64,2048]{2,1,0:T(8,128)(2,1)}, u32[]{:S(2)}, u32[]{:S(2)}) async-start(bf16[16,64,2048]{2,1,0:T(8,128)(2,1)} %bitcast.32), calls=%async_computation | async-start | bytes 8388608 | tf_op jit(solution)/shard_map/all_to_all | solution.py:20
  236.8 31.2 %all-to-all-start.2 = ((bf16[16,64,1024]{2,1,0:T(8,128)(2,1)}), bf16[16,64,1024]{2,1,0:T(8,128)(2,1)S(1)}, u32[]{:S(2)}, u32[]{:S(2)}) async-start(bf16[16,64,1024]{2,1,0:T(8,128)(2,1)} %scatter_fusion.1), calls=%async_computation.2 | async-start | bytes 4194304 | tf_op jit(solution)/shard_map/all_to_all | solution.py:36
  240.6 140.7 %all-reduce.3.cloned.1.call-start = ((), (), s32[]{:S(2)}) async-start(), calls=%async_computation.5 | async-start | bytes 3145728 | tf_op jit(solution)/shard_map/psum | solution.py:46
Sparse Core Ops, SparseCore 0:
  10.1 41.4 all-gather.2
  53.6 104.1 all-gather.4
  270.1 111.0 all-reduce.2
where the time goes:
time: 396 us; the launch traced here: 392 us
  waiting for transfers between devices  187 us (47%)
  local copies, waits for them, and re-layouts  151 us (38%)
  starting transfers between devices  19.9 us (5%)
  between operations  13.8 us (3%)
  matrix products  13.1 us (3%)
  other arithmetic  7.81 us (2%)
    psum x1, waiting for transfers between devices, body(): weight_grad = lax.psum(shard, 'dp')  111 us
    scatter x1, local copies, waits for them, and re-layouts, body(): jnp.zeros((groups, slots, features), jnp.bfloat16).at[target, position]  72.2 us
    scatter x1, local copies, waits for them, and re-layouts, body(): jnp.full((groups, slots), -1, jnp.int32).at[target, position].set(key_row)  71.1 us
    all_gather x1, waiting for transfers between devices, body(): lax.all_gather(value_weight, 'fsdp', axis=0, tiled=True)  50.5 us
    all_to_all x1, waiting for transfers between devices, body(): lax.all_to_all(outgoing, 'fsdp', split_axis=0, concat_axis=0, tiled=True)  22.4 us
    all_to_all x1, starting transfers between devices, body(): lax.all_to_all(out_keys, 'fsdp', split_axis=0, concat_axis=0, tiled=True)  9.6 us
  transfers between devices with their start and end apart: 6, of which 4 were waited for; matrix products, arithmetic and copies ran while one was open for 42% of the time, Pallas kernels for 0%

commit v1 on v0

--- a/solution.py
+++ b/solution.py
@@ -21,7 +21,9 @@
     shard = jnp.sum(arrived.astype(jnp.float32), axis=0)
     back = lax.dot_general(
         all_heads,
-        lax.all_gather(value_weight, "fsdp", axis=0, tiled=True),
+        jnp.concatenate(
+            lax.all_to_all(jnp.stack([value_weight] * lax.axis_size("fsdp")), "fsdp", 0, 0), axis=0
+        ),
         (((1,), (1,)), ((), ())),
         preferred_element_type=jnp.float32,
     )

time: 396 us -> 438 us (1.11)
  waiting for transfers between devices: 187 us -> 236 us
  local copies, waits for them, and re-layouts: 151 us -> 125 us
  blocking collectives: 0 us -> 16.7 us
    all_gather x1 -> x0, waiting for transfers between devices: 50.5 us -> none  [body(): lax.all_gather(value_weight, 'fsdp', axis=0, tiled=True)]
    all_to_all x1, waiting for transfers between devices: 1.26 us -> 44.9 us  [body(): lax.all_to_all(jnp.stack([value_weight] * lax.axis_size('fsdp')), 'fsdp',...]
    all_gather x1, waiting for transfers between devices: 0.02 us -> 43.2 us  [body(): all_heads = lax.all_gather(value_grad, 'tp', axis=1, tiled=True)]
    scatter x1, local copies, waits for them, and re-layouts: 71.1 us -> 43.2 us  [body(): jnp.full((groups, slots), -1, jnp.int32).at[target, position].set(key_row)]
    psum x1, waiting for transfers between devices: 111 us -> 88.7 us  [body(): weight_grad = lax.psum(shard, 'dp')]
    all_to_all x1, waiting for transfers between devices: 22.4 us -> 42.8 us  [body(): lax.all_to_all(outgoing, 'fsdp', split_axis=0, concat_axis=0, tiled=True)]
    all_to_all x0 -> x1, blocking collectives: none -> 16.7 us  [body(): lax.all_to_all(out_keys, 'fsdp', split_axis=0, concat_axis=0, tiled=True)]
    all_to_all x1, waiting for transfers between devices: 0.01 us -> 15.7 us  [body(): lax.all_to_all(pieces, 'fsdp', split_axis=0, concat_axis=0, tiled=True)]
  transfers between devices with their start and end apart: 6 -> 5, of which waited for: 4 -> 5; matrix products, arithmetic and copies ran while one was open for 42% -> 21% of each run, Pallas kernels for 0% -> 0%
where the time goes in v1:
time: 438 us; the launch traced here: 434 us
  waiting for transfers between devices  236 us (54%)
  local copies, waits for them, and re-layouts  125 us (29%)
  starting transfers between devices  22.3 us (5%)
  blocking collectives  16.7 us (4%)
  between operations  14.1 us (3%)
  matrix products  13 us (3%)
  other arithmetic  7.9 us (2%)
    psum x1, waiting for transfers between devices, body(): weight_grad = lax.psum(shard, 'dp')  88.7 us
    scatter x1, local copies, waits for them, and re-layouts, body(): jnp.zeros((groups, slots, features), jnp.bfloat16).at[target, position]  72.2 us
    all_to_all x1, waiting for transfers between devices, body(): lax.all_to_all(jnp.stack([value_weight] * lax.axis_size('fsdp')), 'fsdp',...  44.9 us
    scatter x1, local copies, waits for them, and re-layouts, body(): jnp.full((groups, slots), -1, jnp.int32).at[target, position].set(key_row)  43.2 us
    all_gather x1, waiting for transfers between devices, body(): all_heads = lax.all_gather(value_grad, 'tp', axis=1, tiled=True)  43.2 us
    all_to_all x1, waiting for transfers between devices, body(): lax.all_to_all(outgoing, 'fsdp', split_axis=0, concat_axis=0, tiled=True)  42.8 us
    all_to_all x1, blocking collectives, body(): lax.all_to_all(out_keys, 'fsdp', split_axis=0, concat_axis=0, tiled=True)  16.7 us
    all_to_all x1, waiting for transfers between devices, body(): lax.all_to_all(pieces, 'fsdp', split_axis=0, concat_axis=0, tiled=True)  15.7 us
  transfers between devices with their start and end apart: 5, of which 5 were waited for; matrix products, arithmetic and copies ran while one was open for 21% of the time, Pallas kernels for 0%

profile of v1, /device:TPU:1, one launch (start us, length us, event | category | flops | bytes accessed | tf_op | source)
XLA Modules:
  0.0 434.5 jit_solution(8110806374919963127)
XLA Ops:
  7.2 0.0 copy-start
  7.2 0.8 fusion.4
  8.0 1.1 reduce-window.6
  9.1 0.2 slice_reduce_fusion
  9.3 0.8 fusion.3
  10.1 0.7 or_select_fusion
  10.8 0.0 copy-start.1
  10.9 43.2 %scatter_fusion = s32[16,64]{1,0:T(8,128)S(1)} fusion(s32[16,64]{1,0:T(8,128)S(1)} %broadcast_in_dim.4, s32[512]{0:T(512)S(1)} %bitcast.32, s32[512]{0:T(512)} %param.11), kind=kCustom, calls=%fused_computation | custom fusion | bytes 10240 | tf_op jit(solution)/shard_map/scatter | solution.py:37
  54.1 16.7 %all_to_all.24 = s32[16,1,64]{2,1,0:T(1,128)S(1)} all-to-all(s32[16,1,64]{2,1,0:T(1,128)S(1)} %bitcast.31), channel_id=1, replica_groups=mesh['dp'=8,'fsdp'=16,'tp'=4] {'fsdp'}, dimensions={0} | all-to-all | bytes 8192 | tf_op jit(solution)/shard_map/all_to_all | solution.py:39
  70.8 0.0 copy-done.1
  70.8 2.5 stack.2
  73.3 4.5 %all-to-all-start.2 = ((bf16[16,64,2048]{2,1,0:T(8,128)(2,1)}), bf16[16,64,2048]{2,1,0:T(8,128)(2,1)}, u32[]{:S(2)}, u32[]{:S(2)}) async-start(bf16[16,64,2048]{2,1,0:T(8,128)(2,1)} %stack.2), calls=%async_computation.2 | async-start | bytes 8388608 | tf_op jit(solution)/shard_map/all_to_all | solution.py:25
  77.8 0.0 all-gather.2.cloned.1.call-start
  77.9 0.7 all-gather.2.cloned.1.call-update
  78.6 43.2 %all-gather.2.cloned.1.call-done = bf16[512,2048]{1,0:T(8,128)(2,1)} async-done(((bf16[512,512]{1,0:T(8,128)(2,1)}), bf16[512,2048]{1,0:T(8,128)(2,1)}) %all-gather.2.cloned.1.call-update) | async-done | bytes 2097168 | tf_op jit(solution)/shard_map/all_gather | solution.py:10
  121.8 0.0 copy-done
  121.8 5.9 %convolution_convert_fusion = bf16[1024,2048]{1,0:T(8,128)(2,1)} fusion(bf16[512,1024]{1,0:T(8,128)(2,1)S(1)} %copy-done, bf16[512,2048]{1,0:T(8,128)(2,1)} %all-gather.2.cloned.1.call-done), kind=kOutput, calls=%fused_computation.3 | convolution fusion | flops 2149580800 | bytes 7340032 | tf_op jit(solution)/shard_map/dot_general | solution.py:16
  127.7 44.9 %all-to-all-done.2 = bf16[16,64,2048]{2,1,0:T(8,128)(2,1)} async-done(((bf16[16,64,2048]{2,1,0:T(8,128)(2,1)}), bf16[16,64,2048]{2,1,0:T(8,128)(2,1)}, u32[]{:S(2)}, u32[]{:S(2)}) %all-to-all-start.2) | async-done | bytes 4194336 | tf_op jit(solution)/shard_map/all_to_all | solution.py:25
  172.6 0.0 copy-start.2
  172.6 8.9 %all-to-all-start = ((bf16[16,64,2048]{2,1,0:T(8,128)(2,1)}), bf16[16,64,2048]{2,1,0:T(8,128)(2,1)}, u32[]{:S(2)}, u32[]{:S(2)}) async-start(bf16[16,64,2048]{2,1,0:T(8,128)(2,1)} %bitcast.34), calls=%async_computation | async-start | bytes 8388608 | tf_op jit(solution)/shard_map/all_to_all | solution.py:20
  181.5 0.0 copy-done.2
  181.5 5.2 %add_convert_fusion = bf16[512,1024]{1,0:T(8,128)(2,1)S(1)} fusion(bf16[512,1024]{1,0:T(8,128)(2,1)S(1)} %copy-done.2, bf16[512,2048]{1,0:T(8,128)(2,1)} %all-gather.2.cloned.1.call-done, bf16[1024,2048]{1,0:T(8,128)(2,1)} %bitcast.9), kind=kOutput, calls=%fused_computation.4 | convolution fusion | flops 2149056512 | bytes 8388608 | tf_op jit(solution)/shard_map/dot_general | solution.py:22
  186.7 1.7 broadcast_in_dim.5
  188.4 72.2 %scatter_fusion.1 = bf16[16,64,1024]{2,1,0:T(8,128)(2,1)} fusion(bf16[16,64,1024]{2,1,0:T(8,128)(2,1)} %broadcast_in_dim.5, s32[512]{0:T(512)S(1)} %bitcast.33, bf16[512,1024]{1,0:T(8,128)(2,1)S(1)} %add_convert_fusion), kind=kCustom, calls=%fused_computation.1 | custom fusion | bytes 3149824 | tf_op jit(solution)/shard_map/scatter | solution.py:35
  260.6 15.7 %all-to-all-done = bf16[16,64,2048]{2,1,0:T(8,128)(2,1)} async-done(((bf16[16,64,2048]{2,1,0:T(8,128)(2,1)}), bf16[16,64,2048]{2,1,0:T(8,128)(2,1)}, u32[]{:S(2)}, u32[]{:S(2)}) %all-to-all-start) | async-done | bytes 4194336 | tf_op jit(solution)/shard_map/all_to_all | solution.py:20
  276.3 8.7 %all-to-all-start.3 = ((bf16[16,64,1024]{2,1,0:T(8,128)(2,1)}), bf16[16,64,1024]{2,1,0:T(8,128)(2,1)S(1)}, u32[]{:S(2)}, u32[]{:S(2)}) async-start(bf16[16,64,1024]{2,1,0:T(8,128)(2,1)} %scatter_fusion.1), calls=%async_computation.3 | async-start | bytes 4194304 | tf_op jit(solution)/shard_map/all_to_all | solution.py:38
  285.0 0.0 all-reduce.3.cloned.1.call-start
  285.0 0.5 broadcast.104
  285.5 0.7 reduce.5
  286.2 0.1 eq.48
  286.3 3.8 convert_reduce_fusion
  290.1 42.8 %all-to-all-done.3 = bf16[16,64,1024]{2,1,0:T(8,128)(2,1)S(1)} async-done(((bf16[16,64,1024]{2,1,0:T(8,128)(2,1)}), bf16[16,64,1024]{2,1,0:T(8,128)(2,1)S(1)}, u32[]{:S(2)}, u32[]{:S(2)}) %all-to-all-start.3) | async-done | bytes 2097184 | tf_op jit(solution)/shard_map/all_to_all | solution.py:38
  332.8 1.9 fusion
  334.8 0.0 all-reduce.3.cloned.1.call-update
  334.8 88.7 %all-reduce.3.cloned.1.call-done = (f32[64,2048]{1,0:T(8,128)}, f32[256,1024]{1,0:T(8,128)}) async-done(((f32[64,2048]{1,0:T(8,128)}, f32[256,1024]{1,0:T(8,128)}), (f32[64,2048]{1,0:T(8,128)}, f32[256,1024]{1,0:T(8,128)})) %all-reduce.3.cloned.1.call-update) | async-done | bytes 1572880 | tf_op jit(solution)/shard_map/psum | solution.py:48
  423.5 1.9 copy.17
  425.3 2.3 copy.18
  (4 shorter events, 0.0 us)
Async XLA Ops:
  7.2 114.6 %copy-start = (bf16[512,1024]{1,0:T(8,128)(2,1)S(1)}, bf16[512,1024]{1,0:T(8,128)(2,1)}, u32[]{:S(2)}) copy-start(bf16[512,1024]{1,0:T(8,128)(2,1)} %param.6) | copy-start | bytes 3145732
  10.8 59.9 %copy-start.1 = (bf16[64,2048]{1,0:T(8,128)(2,1)S(1)}, bf16[64,2048]{1,0:T(8,128)(2,1)}, u32[]{:S(2)}) copy-start(bf16[64,2048]{1,0:T(8,128)(2,1)} %param.9) | copy-start | bytes 786436
  73.3 99.3 %all-to-all-start.2 = ((bf16[16,64,2048]{2,1,0:T(8,128)(2,1)}), bf16[16,64,2048]{2,1,0:T(8,128)(2,1)}, u32[]{:S(2)}, u32[]{:S(2)}) async-start(bf16[16,64,2048]{2,1,0:T(8,128)(2,1)} %stack.2), calls=%async_computation.2 | async-start | bytes 8388608 | tf_op jit(solution)/shard_map/all_to_all | solution.py:25
  77.8 43.9 %all-gather.2.cloned.1.call-start = ((), (), s32[]{:S(2)}) async-start(), calls=%async_computation.4 | async-start | bytes 2621440 | tf_op jit(solution)/shard_map/all_gather | solution.py:10
  172.6 9.0 %copy-start.2 = (bf16[512,1024]{1,0:T(8,128)(2,1)S(1)}, bf16[512,1024]{1,0:T(8,128)(2,1)}, u32[]{:S(2)}) copy-start(bf16[512,1024]{1,0:T(8,128)(2,1)} %param.8) | copy-start | bytes 3145732
  172.6 103.7 %all-to-all-start = ((bf16[16,64,2048]{2,1,0:T(8,128)(2,1)}), bf16[16,64,2048]{2,1,0:T(8,128)(2,1)}, u32[]{:S(2)}, u32[]{:S(2)}) async-start(bf16[16,64,2048]{2,1,0:T(8,128)(2,1)} %bitcast.34), calls=%async_computation | async-start | bytes 8388608 | tf_op jit(solution)/shard_map/all_to_all | solution.py:20
  276.3 56.6 %all-to-all-start.3 = ((bf16[16,64,1024]{2,1,0:T(8,128)(2,1)}), bf16[16,64,1024]{2,1,0:T(8,128)(2,1)S(1)}, u32[]{:S(2)}, u32[]{:S(2)}) async-start(bf16[16,64,1024]{2,1,0:T(8,128)(2,1)} %scatter_fusion.1), calls=%async_computation.3 | async-start | bytes 4194304 | tf_op jit(solution)/shard_map/all_to_all | solution.py:38
  285.0 138.5 %all-reduce.3.cloned.1.call-start = ((), (), s32[]{:S(2)}) async-start(), calls=%async_computation.5 | async-start | bytes 3145728 | tf_op jit(solution)/shard_map/psum | solution.py:48
Sparse Core Ops, SparseCore 0:
  80.7 40.9 all-gather.1
  334.9 88.4 all-reduce.2
